TPU v7x, 32 devices: a whole 2x2x4 slice. The times are simulated.
32 devices in a mesh: dp: 16 (over z, y, x), seq: 2 (over core).
Axes of the slice: x: 2, y: 2, z: 4, core: 2. Of those that a mesh axis runs over, the one named last changes fastest.
Arguments:
- block_in: bfloat16 [16, 256, 768], P('dp', 'seq'), may hold values from -6 to 6
- doc_ids: int32 [16, 256], P('dp', 'seq'), may hold values from 0 to 1, as said below
- positions: int32 [16, 256], P('dp', 'seq'), may hold values from 0 to 223, as said below
- ln1_gain: bfloat16 [768], P(('dp', 'seq')), may hold values from 0.5 to 1.5
- ln1_bias: bfloat16 [768], P(('dp', 'seq')), may hold values from -3 to 3
- qkv_weight: bfloat16 [768, 2304], P(('dp', 'seq')), as said below
- qkv_bias: bfloat16 [2304], P(('dp', 'seq')), may hold values from -3 to 3
- attn_weight: bfloat16 [768, 768], P(('dp', 'seq')), may hold values from -0.875 to 0.875
- attn_bias: bfloat16 [768], P(('dp', 'seq')), may hold values from -3 to 3
- ln2_gain: bfloat16 [768], P(('dp', 'seq')), may hold values from 0.5 to 1.5
- ln2_bias: bfloat16 [768], P(('dp', 'seq')), may hold values from -3 to 3
- fc_weight: bfloat16 [768, 3072], P(('dp', 'seq')), may hold values from -0.21875 to 0.21875
- fc_bias: bfloat16 [3072], P(('dp', 'seq')), may hold values from -3 to 3
- proj_weight: bfloat16 [3072, 768], P(('dp', 'seq')), may hold values from -0.109375 to 0.109375
- proj_bias: bfloat16 [768], P(('dp', 'seq')), may hold values from -3 to 3
- grad_out: bfloat16 [16, 256, 768], P('dp', 'seq'), may hold values from -6 to 6
Outputs:
- block_out: bfloat16 [16, 256, 768], P('dp', 'seq')
- grad_in: bfloat16 [16, 256, 768], P('dp', 'seq')
- grad_ln1_gain: float32 [768], P(('dp', 'seq'))
- grad_ln1_bias: float32 [768], P(('dp', 'seq'))
- grad_qkv_weight: float32 [768, 2304], P(('dp', 'seq'))
- grad_qkv_bias: float32 [2304], P(('dp', 'seq'))
- grad_attn_weight: float32 [768, 768], P(('dp', 'seq'))
- grad_attn_bias: float32 [768], P(('dp', 'seq'))
- grad_ln2_gain: float32 [768], P(('dp', 'seq'))
- grad_ln2_bias: float32 [768], P(('dp', 'seq'))
- grad_fc_weight: float32 [768, 3072], P(('dp', 'seq'))
- grad_fc_bias: float32 [3072], P(('dp', 'seq'))
- grad_proj_weight: float32 [3072, 768], P(('dp', 'seq'))
- grad_proj_bias: float32 [768], P(('dp', 'seq'))
Inputs may be any that keep to these rules, and one draw needn't show every extreme that they name: `doc_ids`: each row holds two documents: id 0 on its first tokens and id 1 on the rest; the first has 32 to 224 tokens. `positions`: each token's index within its document. `qkv_weight`: columns are the query, key and value projections in that order, each with its heads side by side.
All inputs are finite; a program needn't handle non-finite values.
Results may differ from a plain program's by a relative error of at most 0.009.
Values may be sent and summed in bfloat16 or wider, within the bound.
No kernel may reach another device: no remote copies, remote signals or barrier semaphores. Data moves between devices by JAX's collectives and lax.ppermute only.
A program may use at most 192 MiB of HBM per device.

v0:
```python
import math
import jax
import jax.numpy as jnp
from jax import lax
from jax.sharding import PartitionSpec as P

HEADS = 12
HEAD = 64
ROT = 16
EPSILON = 1e-05
ROOT_HALF = 1.0 / math.sqrt(2.0)
ROOT_TWO_PI = 1.0 / math.sqrt(2.0 * math.pi)


def from_behind(shard, axis, by):
    devices = lax.axis_size(axis)
    pairs = [(i, i + by) for i in range(devices) if 0 <= i + by < devices]
    return lax.ppermute(shard, axis, pairs)


def layer_norm(values):
    centred = values - jnp.mean(values, -1, keepdims=True)
    inverse = lax.rsqrt(jnp.mean(centred * centred, -1, keepdims=True) + EPSILON)
    return (centred * inverse, inverse)


def norm_back(upstream, normed, inverse, gain_vec):
    scaled = upstream * gain_vec.astype(jnp.float32)
    return inverse * (
        scaled
        - jnp.mean(scaled, -1, keepdims=True)
        - normed * jnp.mean(scaled * normed, -1, keepdims=True)
    )


def gelu_slope(pre_act):
    return (
        0.5 * (1.0 + lax.erf(pre_act * ROOT_HALF))
        + pre_act * jnp.exp(-0.5 * pre_act * pre_act) * ROOT_TWO_PI
    )


def tables(token_pos):
    half_rot = ROT // 2
    frequency = 10000.0 ** (-(jnp.arange(half_rot).astype(jnp.float32) * 2.0 / ROT))
    angles = token_pos.astype(jnp.float32)[:, None] * frequency[None, :]
    return (jnp.cos(angles)[:, None, :], jnp.sin(angles)[:, None, :])


def rotate(heads, cos_table, sine_table):
    half_rot = ROT // 2
    first = heads[..., :half_rot]
    second = heads[..., half_rot:ROT]
    return jnp.concatenate(
        [
            first * cos_table - second * sine_table,
            second * cos_table + first * sine_table,
            heads[..., ROT:],
        ],
        -1,
    )


def unrotate(heads, cos_table, sine_table):
    half_rot = ROT // 2
    first = heads[..., :half_rot]
    second = heads[..., half_rot:ROT]
    return jnp.concatenate(
        [
            first * cos_table + second * sine_table,
            second * cos_table - first * sine_table,
            heads[..., ROT:],
        ],
        -1,
    )


def local(
    block_in,
    doc_ids,
    positions,
    ln1_gain,
    ln1_bias,
    qkv_weight,
    qkv_bias,
    attn_weight,
    attn_bias,
    ln2_gain,
    ln2_bias,
    fc_weight,
    fc_bias,
    proj_weight,
    proj_bias,
    grad_out,
):
    gathered = (
        lax.all_gather(ln1_gain, ("dp", "seq"), axis=0, tiled=True),
        lax.all_gather(ln1_bias, ("dp", "seq"), axis=0, tiled=True),
        lax.all_gather(qkv_weight, ("dp", "seq"), axis=0, tiled=True),
        lax.all_gather(qkv_bias, ("dp", "seq"), axis=0, tiled=True),
        lax.all_gather(attn_weight, ("dp", "seq"), axis=0, tiled=True),
        lax.all_gather(attn_bias, ("dp", "seq"), axis=0, tiled=True),
        lax.all_gather(ln2_gain, ("dp", "seq"), axis=0, tiled=True),
        lax.all_gather(ln2_bias, ("dp", "seq"), axis=0, tiled=True),
        lax.all_gather(fc_weight, ("dp", "seq"), axis=0, tiled=True),
        lax.all_gather(fc_bias, ("dp", "seq"), axis=0, tiled=True),
        lax.all_gather(proj_weight, ("dp", "seq"), axis=0, tiled=True),
        lax.all_gather(proj_bias, ("dp", "seq"), axis=0, tiled=True),
    )
    (
        norm1_gain,
        norm1_bias,
        qkv_mat,
        qkv_vec,
        out_mat,
        out_vec,
        norm2_gain,
        norm2_bias,
        fc_mat,
        fc_vec,
        proj_mat,
        proj_vec,
    ) = gathered
    row_count, local_len, model_width = block_in.shape
    tokens = row_count * local_len
    offset = lax.axis_index("seq") * local_len
    score_scale = HEAD ** (-0.5)
    float_type = jnp.float32
    inputs = block_in.reshape(tokens, model_width).astype(float_type)
    normed, inverse = layer_norm(inputs)
    acts1 = (normed * norm1_gain.astype(float_type) + norm1_bias.astype(float_type)).astype(
        jnp.bfloat16
    )
    acts2 = (normed * norm2_gain.astype(float_type) + norm2_bias.astype(float_type)).astype(
        jnp.bfloat16
    )
    projected = jnp.dot(acts1, qkv_mat, preferred_element_type=float_type) + qkv_vec.astype(
        float_type
    )
    cos_table, sine_table = tables(positions.reshape(tokens))
    queries = rotate(
        projected[:, :model_width].reshape(tokens, HEADS, HEAD), cos_table, sine_table
    ).astype(jnp.bfloat16)
    keys_own = (
        rotate(
            projected[:, model_width : 2 * model_width].reshape(tokens, HEADS, HEAD),
            cos_table,
            sine_table,
        )
        .astype(jnp.bfloat16)
        .reshape(row_count, local_len, model_width)
    )
    values_own = (
        projected[:, 2 * model_width :]
        .astype(jnp.bfloat16)
        .reshape(row_count, local_len, model_width)
    )
    docs_own = doc_ids.astype(jnp.bfloat16)
    keys_prev, values_prev, docs_prev = from_behind((keys_own, values_own, docs_own), "seq", 1)
    keys_all = jnp.concatenate([keys_prev, keys_own], 1).reshape(
        row_count, 2 * local_len, HEADS, HEAD
    )
    values_all = jnp.concatenate([values_prev, values_own], 1).reshape(
        row_count, 2 * local_len, HEADS, HEAD
    )
    docs_all = jnp.concatenate([docs_prev, docs_own], 1)
    query_heads = queries.reshape(row_count, local_len, HEADS, HEAD)
    query_index = offset + jnp.arange(local_len)
    key_index = offset - local_len + jnp.arange(2 * local_len)
    allowed = (key_index[None, :] <= query_index[:, None]) & (key_index[None, :] >= 0)
    allowed = (allowed[None] & (docs_all[:, None, :] == docs_own[:, :, None]))[:, None]

    def scores_of():
        raw_scores = (
            jnp.einsum("rqhd,rkhd->rhqk", query_heads, keys_all, preferred_element_type=float_type)
            * score_scale
        )
        return jnp.where(allowed, raw_scores, -jnp.inf)

    scores = scores_of()
    row_max = jnp.max(scores, -1, keepdims=True)
    logsum = row_max + jnp.log(jnp.sum(jnp.exp(scores - row_max), -1, keepdims=True))
    probs = jnp.exp(scores - logsum).astype(jnp.bfloat16)
    context = (
        jnp.einsum("rhqk,rkhd->rqhd", probs, values_all, preferred_element_type=float_type)
        .astype(jnp.bfloat16)
        .reshape(tokens, model_width)
    )
    pre_act = jnp.dot(acts2, fc_mat, preferred_element_type=float_type) + fc_vec.astype(float_type)
    hidden = jax.nn.gelu(pre_act, approximate=False).astype(jnp.bfloat16)
    attn_out = jnp.dot(context, out_mat, preferred_element_type=float_type) + out_vec.astype(
        float_type
    )
    mlp_out = jnp.dot(hidden, proj_mat, preferred_element_type=float_type) + proj_vec.astype(
        float_type
    )
    block_out = (
        (inputs + attn_out + mlp_out)
        .astype(jnp.bfloat16)
        .reshape(row_count, local_len, model_width)
    )
    (
        norm1_gain,
        norm1_bias,
        qkv_mat,
        qkv_vec,
        out_mat,
        out_vec,
        norm2_gain,
        norm2_bias,
        fc_mat,
        fc_vec,
        proj_mat,
        proj_vec,
    ) = gathered
    upstream_b = grad_out.reshape(tokens, model_width)
    upstream = upstream_b.astype(float_type)
    grad_proj_bias = jnp.sum(upstream, 0)
    grad_proj_weight = jnp.einsum(
        "nf,nd->fd", hidden, upstream_b, preferred_element_type=float_type
    )
    d_pre = jnp.einsum(
        "nd,fd->nf", upstream_b, proj_mat, preferred_element_type=float_type
    ) * gelu_slope(pre_act)
    grad_fc_bias = jnp.sum(d_pre, 0)
    d_pre_b = d_pre.astype(jnp.bfloat16)
    grad_fc_weight = jnp.einsum("nd,nf->df", acts2, d_pre_b, preferred_element_type=float_type)
    d_acts2 = jnp.einsum("nf,df->nd", d_pre_b, fc_mat, preferred_element_type=float_type)
    grad_ln2_gain = jnp.sum(d_acts2 * normed, 0)
    grad_ln2_bias = jnp.sum(d_acts2, 0)
    grad_attn_bias = jnp.sum(upstream, 0)
    grad_attn_weight = jnp.einsum(
        "nc,nd->cd", context, upstream_b, preferred_element_type=float_type
    )
    d_context = jnp.einsum(
        "nd,cd->nc", upstream_b, out_mat, preferred_element_type=float_type
    ).astype(jnp.bfloat16)
    d_ctx_heads = d_context.reshape(row_count, local_len, HEADS, HEAD)
    row_dot = jnp.sum(
        d_ctx_heads.astype(float_type)
        * context.reshape(row_count, local_len, HEADS, HEAD).astype(float_type),
        -1,
    )
    scores = scores_of()
    weights_full = jnp.exp(scores - logsum)
    d_weights = jnp.einsum(
        "rqhd,rkhd->rhqk", d_ctx_heads, values_all, preferred_element_type=float_type
    )
    d_scores = (
        weights_full * (d_weights - jnp.transpose(row_dot, (0, 2, 1))[..., None]) * score_scale
    ).astype(jnp.bfloat16)
    d_query = jnp.einsum("rhqk,rkhd->rqhd", d_scores, keys_all, preferred_element_type=float_type)
    d_keys = jnp.einsum(
        "rhqk,rqhd->rkhd", d_scores, query_heads, preferred_element_type=float_type
    ).reshape(row_count, 2 * local_len, model_width)
    d_values = jnp.einsum(
        "rhqk,rqhd->rkhd", probs, d_ctx_heads, preferred_element_type=float_type
    ).reshape(row_count, 2 * local_len, model_width)
    back_keys, back_values = (
        from_behind(d_keys[:, :local_len].astype(jnp.bfloat16), "seq", -1).astype(jnp.float32),
        from_behind(d_values[:, :local_len].astype(jnp.bfloat16), "seq", -1).astype(jnp.float32),
    )
    d_keys_own = (d_keys[:, local_len:] + back_keys).reshape(tokens, HEADS, HEAD)
    d_values_own = (d_values[:, local_len:] + back_values).reshape(tokens, model_width)
    d_projected = jnp.concatenate(
        [
            unrotate(d_query.reshape(tokens, HEADS, HEAD), cos_table, sine_table).reshape(
                tokens, model_width
            ),
            unrotate(d_keys_own, cos_table, sine_table).reshape(tokens, model_width),
            d_values_own,
        ],
        1,
    )
    grad_qkv_bias = jnp.sum(d_projected, 0)
    d_proj_b = d_projected.astype(jnp.bfloat16)
    grad_qkv_weight = jnp.einsum("nd,ne->de", acts1, d_proj_b, preferred_element_type=float_type)
    d_acts1 = jnp.einsum("ne,de->nd", d_proj_b, qkv_mat, preferred_element_type=float_type)
    grad_ln1_gain = jnp.sum(d_acts1 * normed, 0)
    grad_ln1_bias = jnp.sum(d_acts1, 0)
    grad_in = (
        (
            upstream
            + norm_back(d_acts1, normed, inverse, norm1_gain)
            + norm_back(d_acts2, normed, inverse, norm2_gain)
        )
        .astype(jnp.bfloat16)
        .reshape(row_count, local_len, model_width)
    )
    summed = (
        lax.psum_scatter(grad_ln1_gain, ("dp", "seq"), scatter_dimension=0, tiled=True),
        lax.psum_scatter(grad_ln1_bias, ("dp", "seq"), scatter_dimension=0, tiled=True),
        lax.psum_scatter(grad_qkv_weight, ("dp", "seq"), scatter_dimension=0, tiled=True),
        lax.psum_scatter(grad_qkv_bias, ("dp", "seq"), scatter_dimension=0, tiled=True),
        lax.psum_scatter(grad_attn_weight, ("dp", "seq"), scatter_dimension=0, tiled=True),
        lax.psum_scatter(grad_attn_bias, ("dp", "seq"), scatter_dimension=0, tiled=True),
        lax.psum_scatter(grad_ln2_gain, ("dp", "seq"), scatter_dimension=0, tiled=True),
        lax.psum_scatter(grad_ln2_bias, ("dp", "seq"), scatter_dimension=0, tiled=True),
        lax.psum_scatter(grad_fc_weight, ("dp", "seq"), scatter_dimension=0, tiled=True),
        lax.psum_scatter(grad_fc_bias, ("dp", "seq"), scatter_dimension=0, tiled=True),
        lax.psum_scatter(grad_proj_weight, ("dp", "seq"), scatter_dimension=0, tiled=True),
        lax.psum_scatter(grad_proj_bias, ("dp", "seq"), scatter_dimension=0, tiled=True),
    )
    return (
        block_out,
        grad_in,
        summed[0],
        summed[1],
        summed[2],
        summed[3],
        summed[4],
        summed[5],
        summed[6],
        summed[7],
        summed[8],
        summed[9],
        summed[10],
        summed[11],
    )


def solution(mesh):
    placed = (
        P("dp", "seq", None),
        P("dp", "seq"),
        P("dp", "seq"),
        P(("dp", "seq")),
        P(("dp", "seq")),
        P(("dp", "seq"), None),
        P(("dp", "seq")),
        P(("dp", "seq"), None),
        P(("dp", "seq")),
        P(("dp", "seq")),
        P(("dp", "seq")),
        P(("dp", "seq"), None),
        P(("dp", "seq")),
        P(("dp", "seq"), None),
        P(("dp", "seq")),
        P("dp", "seq", None),
    )
    return jax.shard_map(
        local,
        mesh=mesh,
        in_specs=placed,
        out_specs=(
            P("dp", "seq", None),
            P("dp", "seq", None),
            P(("dp", "seq")),
            P(("dp", "seq")),
            P(("dp", "seq"), None),
            P(("dp", "seq")),
            P(("dp", "seq"), None),
            P(("dp", "seq")),
            P(("dp", "seq")),
            P(("dp", "seq")),
            P(("dp", "seq"), None),
            P(("dp", "seq")),
            P(("dp", "seq"), None),
            P(("dp", "seq")),
        ),
        check_vma=False,
    )
```

profile of v0, /device:TPU:0, one launch (start us, length us, event | category | flops | bytes accessed | tf_op | source)
XLA Modules:
  0.0 778.8 jit_solution(5045780520184419339)
XLA Ops:
  7.2 0.7 all-gather.7.cloned.1.call-update
  8.0 0.7 all-gather.5.cloned.1.call-update
  8.7 0.7 all-gather.9.cloned.1.call-update
  9.5 0.5 all-gather.11.cloned.1.call-update
  10.0 0.7 convert_bitcast_fusion.2
  10.7 2.4 collective-permute-start.1
  13.1 0.8 dynamic-update-slice
  14.0 0.8 dynamic-update-slice.1
  14.8 0.8 dynamic-update-slice.7
  15.6 0.8 dynamic-update-slice.4
  16.5 0.8 dynamic-update-slice.5
  17.3 0.8 dynamic-update-slice.3
  18.1 0.8 dynamic-update-slice.2
  19.0 0.8 dynamic-update-slice.6
  19.8 42.1 %all-reduce.16 = (bf16[3072]{0:T(1024)(128)(2,1)}, bf16[768]{0:T(1024)(128)(2,1)}, bf16[768]{0:T(1024)(128)(2,1)}, bf16[768]{0:T(1024)(128)(2,1)}, bf16[2304]{0:...) all-reduce(bf16[3072]{0:T(1024)(128)(2,1)S(1)} %dynamic-update-slic, ...), channel_id=1, replica_groups=mesh['dp'=16,'seq'=2] {'dp','seq'}, use_global_device_ids=true, to_apply=%add.6 | all-reduce | flops 9984 | bytes 39936
  62.0 1.0 convert_reduce_fusion.1
  63.0 1.1 fusion.46
  64.1 0.7 convert_bitcast_fusion.1
  65.0 0.7 compare_and_fusion
  65.7 2.0 all-gather.7.cloned.1.call-done
  67.8 1.9 convolution_convert_fusion
  69.8 59.9 %all-gather.5.cloned.1.call-done = bf16[768,2304]{1,0:T(8,128)(2,1)} async-done(((bf16[24,2304]{1,0:T(8,128)(2,1)}), bf16[768,2304]{1,0:T(8,128)(2,1)}) %all-gather.5.cloned.1.call-update) | async-done | bytes 3538960 | tf_op jit(solution)/shard_map/all_gather | solution.py:99
  129.7 2.7 convolution_add_fusion
  132.9 2.2 collective-permute-start
  135.4 1.3 collective-permute-start.2
  136.9 0.8 collective-permute-done.2
  137.8 1.3 fusion.77
  139.0 0.5 exponential_reduce_fusion
  139.6 1.1 multiply_reduce_fusion
  140.7 1.8 fusion.57
  142.8 0.5 copy-done.14
  143.2 0.7 multiply_convert_fusion
  144.3 0.5 fusion.52
  144.8 1.3 collective-permute-start.4
  146.1 1.3 collective-permute-start.3
  147.4 0.4 convolution_bitcast_fusion
  147.9 1.6 collective-permute-done.3
  149.7 0.5 copy-done.16
  150.2 4.1 fusion.68
  154.6 0.4 copy-done.23
  155.0 40.0 %all-gather.9.cloned.1.call-done = bf16[768,3072]{1,0:T(8,128)(2,1)} async-done(((bf16[24,3072]{1,0:T(8,128)(2,1)}), bf16[768,3072]{1,0:T(8,128)(2,1)}) %all-gather.9.cloned.1.call-update) | async-done | bytes 4718608 | tf_op jit(solution)/shard_map/all_gather | solution.py:105
  195.1 7.6 fusion.2
  202.7 57.1 %all-gather.11.cloned.1.call-done = bf16[3072,768]{1,0:T(8,128)(2,1)} async-done(((bf16[96,768]{1,0:T(8,128)(2,1)}), bf16[3072,768]{1,0:T(8,128)(2,1)}) %all-gather.11.cloned.1.call-update) | async-done | bytes 4718608 | tf_op jit(solution)/shard_map/all_gather | solution.py:107
  259.8 4.6 fusion.78
  264.4 5.1 fusion.48
  269.6 5.1 fusion.55
  274.7 0.6 copy-done.21
  275.7 4.2 fusion.50
  279.9 1.5 fusion.44
  281.5 1.0 convert_reduce_fusion
  282.5 40.1 %all-reduce.15 = (f32[768]{0:T(1024)S(1)}, f32[768]{0:T(1024)S(1)}, f32[2304]{0:T(1024)S(1)}, f32[768]{0:T(1024)S(1)}, f32[768]{0:T(1024)S(1)}, /*index=5*/f32[768]{0:T(1024)S(1)}, f32[3072]{0:T(1024)S(1)}) all-reduce(f32[768]{0:T(1024)S(1)} %get-tuple-element.16, ...), channel_id=2, replica_groups=mesh['dp'=16,'seq'=2] {'dp','seq'}, use_global_device_ids=true, to_apply=%region_10.11.clone | all-reduce | flops 9216 | bytes 73728
  322.7 0.6 dynamic-slice
  323.3 0.6 dynamic-slice.1
  323.9 0.6 dynamic-slice.4
  324.5 0.6 dynamic-slice.5
  325.1 0.6 dynamic-slice.6
  325.7 0.6 dynamic-slice.2
  326.2 3.2 convolution_add_fusion.3
  329.5 1.0 fusion.18
  330.6 32.9 %reduce-scatter.7.cloned.1.call-done = f32[24,768]{1,0:T(8,128)} async-done(((f32[768,768]{1,0:T(8,128)}), f32[24,768]{1,0:T(8,128)}) %reduce-scatter.7.cloned.1.call-update) | async-done | bytes 73744 | tf_op jit(solution)/shard_map/reduce_scatter | solution.py:295
  363.5 124.8 %reduce-scatter.5.cloned.1.call-done = f32[24,2304]{1,0:T(8,128)} async-done(((f32[768,2304]{1,0:T(8,128)}), f32[24,2304]{1,0:T(8,128)}) %reduce-scatter.5.cloned.1.call-update) | async-done | bytes 221200 | tf_op jit(solution)/shard_map/reduce_scatter | solution.py:293
  488.3 141.6 %reduce-scatter.9.cloned.1.call-done = f32[24,3072]{1,0:T(8,128)} async-done(((f32[768,3072]{1,0:T(8,128)}), f32[24,3072]{1,0:T(8,128)}) %reduce-scatter.9.cloned.1.call-update) | async-done | bytes 294928 | tf_op jit(solution)/shard_map/reduce_scatter | solution.py:299
  629.9 141.6 %reduce-scatter.11.cloned.1.call-done = f32[96,768]{1,0:T(8,128)} async-done(((f32[3072,768]{1,0:T(8,128)}), f32[96,768]{1,0:T(8,128)}) %reduce-scatter.11.cloned.1.call-update) | async-done | bytes 294928 | tf_op jit(solution)/shard_map/reduce_scatter | solution.py:301
  771.5 0.5 copy.62
  (119 shorter events, 3.1 us)
Async XLA Ops:
  7.2 60.6 %all-gather.7.cloned.1.call-start = ((), (), s32[]{:S(2)}) async-start(), calls=%async_computation.5 | async-start | bytes 1216512 | tf_op jit(solution)/shard_map/all_gather | solution.py:101
  7.9 121.8 %copy-start = (bf16[1,128,768]{2,1,0:T(8,128)(2,1)S(1)}, bf16[1,128,768]{2,1,0:T(8,128)(2,1)}, u32[]{:S(2)}) copy-start(bf16[1,128,768]{2,1,0:T(8,128)(2,1)} %param.16) | copy-start | bytes 589828
  7.9 121.8 %all-gather.5.cloned.1.call-start = ((), (), s32[]{:S(2)}) async-start(), calls=%async_computation.4 | async-start | bytes 3649536 | tf_op jit(solution)/shard_map/all_gather | solution.py:99
  8.7 186.4 %all-gather.9.cloned.1.call-start = ((), (), s32[]{:S(2)}) async-start(), calls=%async_computation.6 | async-start | bytes 4866048 | tf_op jit(solution)/shard_map/all_gather | solution.py:105
  9.4 250.4 %all-gather.11.cloned.1.call-start = ((), (), s32[]{:S(2)}) async-start(), calls=%async_computation.7 | async-start | bytes 4866048 | tf_op jit(solution)/shard_map/all_gather | solution.py:107
  10.0 353.5 %reduce-scatter.7.cloned.1.call-start = ((), (), s32[]{:S(2)}) async-start(), calls=%async_computation.9 | async-start | bytes 2433024 | tf_op jit(solution)/shard_map/reduce_scatter | solution.py:295
  10.7 54.3 %collective-permute-start.1 = (bf16[1,128]{1,0:T(2,128)(2,1)S(1)}, bf16[1,128]{1,0:T(2,128)(2,1)S(1)}, u32[]{:S(2)}, u32[]{:S(2)}) collective-permute-start(bf16[1,128]{1,0:T(2,128)(2,1)S(1)} %get-tuple-element.60), channel_id=1, source_target_pairs={{0,1},{2,3},{4,5},{6,7},{8,9},{10,11},{12,13},{14,15},{16,17},{18,... | collective-permute-start | bytes 776 | tf_op jit(solution)/shard_map/ppermute | solution.py:18
  63.0 66.7 %copy-start.15 = (f32[128]{0:T(128)}, f32[128]{0:T(128)S(1)}, u32[]{:S(2)}) copy-start(f32[128]{0:T(128)S(1)} %broadcast_multiply_fusion.4) | copy-start | bytes 1540
  64.8 64.9 %copy-start.17 = (f32[128]{0:T(128)}, f32[128]{0:T(128)S(1)}, u32[]{:S(2)}) copy-start(f32[128]{0:T(128)S(1)} %add_rsqrt_fusion) | copy-start | bytes 1540
  64.9 70.4 %copy-start.10 = (f32[128,8]{0,1:T(8,128)}, f32[128,8]{0,1:T(8,128)S(1)}, u32[]{:S(2)}) copy-start(f32[128,8]{0,1:T(8,128)S(1)} %get-tuple-element.57) | copy-start | bytes 12292
  64.9 70.4 %copy-start.12 = (f32[128,8]{0,1:T(8,128)}, f32[128,8]{0,1:T(8,128)S(1)}, u32[]{:S(2)}) copy-start(f32[128,8]{0,1:T(8,128)S(1)} %get-tuple-element.58) | copy-start | bytes 12292
  132.9 3.8 collective-permute-start
  135.3 3.7 copy-start.6
  135.4 3.7 copy-start.8
  135.4 2.4 collective-permute-start.2
  136.7 2.3 copy-start.4
  137.8 1.3 copy-start.24
  139.6 1.1 copy-start.3
  142.5 0.7 copy-start.14
  142.6 345.8 %reduce-scatter.5.cloned.1.call-start = ((), (), s32[]{:S(2)}) async-start(), calls=%async_computation.8 | async-start | bytes 7299072 | tf_op jit(solution)/shard_map/reduce_scatter | solution.py:293
  144.2 3.2 copy-start.5
  144.2 3.2 copy-start.7
  144.2 3.2 copy-start.9
  144.2 3.2 copy-start.25
  144.8 4.7 copy-start.11
  144.8 4.7 copy-start.13
  144.8 4.9 collective-permute-start.4
  146.1 3.3 collective-permute-start.3
  149.5 0.7 copy-start.16
  149.5 0.7 copy-start.18
  154.3 0.7 copy-start.23
  154.3 0.7 copy-start.22
  154.3 0.7 copy-start.19
  154.4 475.5 %reduce-scatter.9.cloned.1.call-start = ((), (), s32[]{:S(2)}) async-start(), calls=%async_computation.10 | async-start | bytes 9732096 | tf_op jit(solution)/shard_map/reduce_scatter | solution.py:299
  269.5 502.0 %reduce-scatter.11.cloned.1.call-start = ((), (), s32[]{:S(2)}) async-start(), calls=%async_computation.11 | async-start | bytes 9732096 | tf_op jit(solution)/shard_map/reduce_scatter | solution.py:301
  274.6 0.7 copy-start.21
  274.6 0.7 copy-start.20
  275.7 4.2 copy-start.2
  323.3 448.2 %copy-start.26 = (f32[24]{0:T(128)}, f32[24]{0:T(128)S(1)}, u32[]{:S(2)}) copy-start(f32[24]{0:T(128)S(1)} %dynamic-slice.3) | copy-start | bytes 292
  326.2 3.2 copy-start.1
Sparse Core Ops, SparseCore 0:
  10.9 56.8 all-gather.6
  70.7 59.0 all-gather.4
  132.6 62.3 all-gather.8
  197.8 61.9 all-gather.10
  265.5 97.9 reduce-scatter.6
  369.6 118.6 reduce-scatter.4
  494.8 135.0 reduce-scatter.8
  636.3 135.1 reduce-scatter.10
where the time goes:
time: 780 us; the launch traced here: 779 us
  waiting for transfers between devices  605 us (78%)
  blocking collectives  82.2 us (11%)
  matrix products  47.1 us (6%)
  between operations  14.8 us (2%)
  local copies, waits for them, and re-layouts  14.1 us (2%)
  starting transfers between devices  8.92 us (1%)
    reduce_scatter x1, waiting for transfers between devices, local(): lax.psum_scatter(grad_proj_weight, ('dp', 'seq'), scatter_dimension=0, ti...  142 us
    reduce_scatter x1, waiting for transfers between devices, local(): lax.psum_scatter(grad_fc_weight, ('dp', 'seq'), scatter_dimension=0, tile...  142 us
    reduce_scatter x1, waiting for transfers between devices, local(): lax.psum_scatter(grad_qkv_weight, ('dp', 'seq'), scatter_dimension=0, til...  125 us
    unnamed x2, blocking collectives  82.2 us
    all_gather x1, waiting for transfers between devices, local(): lax.all_gather(qkv_weight, ('dp', 'seq'), axis=0, tiled=True)  59.9 us
    all_gather x1, waiting for transfers between devices, local(): lax.all_gather(proj_weight, ('dp', 'seq'), axis=0, tiled=True)  57.1 us
    all_gather x1, waiting for transfers between devices, local(): lax.all_gather(fc_weight, ('dp', 'seq'), axis=0, tiled=True)  40 us
    reduce_scatter x1, waiting for transfers between devices, local(): lax.psum_scatter(grad_attn_weight, ('dp', 'seq'), scatter_dimension=0, ti...  32.9 us
  transfers between devices with their start and end apart: 13, of which 10 were waited for; matrix products, arithmetic and copies ran while one was open for 8% of the time, Pallas kernels for 0%

commit v1 on v0

--- a/solution.py
+++ b/solution.py
@@ -10,6 +10,11 @@
 EPSILON = 1e-05
 ROOT_HALF = 1.0 / math.sqrt(2.0)
 ROOT_TWO_PI = 1.0 / math.sqrt(2.0 * math.pi)
+
+
+def tiled_gather(x, axis, dim):
+    copies = jnp.concatenate([x] * lax.axis_size(axis), axis=dim)
+    return lax.all_to_all(copies, axis, dim, dim, tiled=True)
 
 
 def from_behind(shard, axis, by):
@@ -104,7 +109,7 @@
         lax.all_gather(ln2_bias, ("dp", "seq"), axis=0, tiled=True),
         lax.all_gather(fc_weight, ("dp", "seq"), axis=0, tiled=True),
         lax.all_gather(fc_bias, ("dp", "seq"), axis=0, tiled=True),
-        lax.all_gather(proj_weight, ("dp", "seq"), axis=0, tiled=True),
+        tiled_gather(proj_weight, ("dp", "seq"), 0),
         lax.all_gather(proj_bias, ("dp", "seq"), axis=0, tiled=True),
     )
     (

time: 780 us -> 750 us (0.962)
  waiting for transfers between devices: 605 us -> 544 us
  local copies, waits for them, and re-layouts: 14.1 us -> 43.3 us
    all_gather x1 -> x0, waiting for transfers between devices: 57.1 us -> none  [local(): lax.all_gather(proj_weight, ('dp', 'seq'), axis=0, tiled=True)]
    all_to_all x0 -> x1, waiting for transfers between devices: none -> 46.3 us  [tiled_gather(): return lax.all_to_all(copies, axis, dim, dim, tiled=True)]
    reduce_scatter x1, waiting for transfers between devices: 32.9 us -> 0.01 us  [local(): lax.psum_scatter(grad_attn_weight, ('dp', 'seq'), scatter_dimension=0, ti...]
    unnamed x78 -> x97, local copies, waits for them, and re-layouts: 12.9 us -> 37.3 us
    all_gather x1, waiting for transfers between devices: 40 us -> 58 us  [local(): lax.all_gather(fc_weight, ('dp', 'seq'), axis=0, tiled=True)]
    reduce_scatter x1, waiting for transfers between devices: 125 us -> 108 us  [local(): lax.psum_scatter(grad_qkv_weight, ('dp', 'seq'), scatter_dimension=0, til...]
    all_gather x1, waiting for transfers between devices: 59.9 us -> 44.8 us  [local(): lax.all_gather(qkv_weight, ('dp', 'seq'), axis=0, tiled=True)]
  transfers between devices with their start and end apart: 13 -> 13, of which waited for: 10 -> 8; matrix products, arithmetic and copies ran while one was open for 8% -> 12% of each run, Pallas kernels for 0% -> 0%
where the time goes in v1:
time: 750 us; the launch traced here: 749 us
  waiting for transfers between devices  544 us (73%)
  blocking collectives  80.7 us (11%)
  matrix products  48.1 us (6%)
  local copies, waits for them, and re-layouts  43.3 us (6%)
  between operations  14.7 us (2%)
  starting transfers between devices  13.1 us (2%)
    reduce_scatter x1, waiting for transfers between devices, local(): lax.psum_scatter(grad_proj_weight, ('dp', 'seq'), scatter_dimension=0, ti...  142 us
    reduce_scatter x1, waiting for transfers between devices, local(): lax.psum_scatter(grad_fc_weight, ('dp', 'seq'), scatter_dimension=0, tile...  141 us
    reduce_scatter x1, waiting for transfers between devices, local(): lax.psum_scatter(grad_qkv_weight, ('dp', 'seq'), scatter_dimension=0, til...  108 us
    unnamed x2, blocking collectives  80.7 us
    all_gather x1, waiting for transfers between devices, local(): lax.all_gather(fc_weight, ('dp', 'seq'), axis=0, tiled=True)  58 us
    all_to_all x1, waiting for transfers between devices, tiled_gather(): return lax.all_to_all(copies, axis, dim, dim, tiled=True)  46.3 us
    all_gather x1, waiting for transfers between devices, local(): lax.all_gather(qkv_weight, ('dp', 'seq'), axis=0, tiled=True)  44.8 us
    unnamed x97, local copies, waits for them, and re-layouts  37.3 us
  transfers between devices with their start and end apart: 13, of which 8 were waited for; matrix products, arithmetic and copies ran while one was open for 12% of the time, Pallas kernels for 0%

profile of v1, /device:TPU:0, one launch (start us, length us, event | category | flops | bytes accessed | tf_op | source)
XLA Modules:
  0.0 748.7 jit_solution(14867148647906645607)
XLA Ops:
  7.2 0.7 all-gather.6.cloned.1.call-update
  8.0 0.7 all-gather.4.cloned.1.call-update
  8.7 0.7 all-gather.8.cloned.1.call-update
  10.1 2.4 collective-permute-start.1
  12.5 0.8 dynamic-update-slice.5
  13.4 0.8 dynamic-update-slice.4
  14.2 0.8 dynamic-update-slice.7
  15.0 0.8 dynamic-update-slice.1
  15.9 0.8 dynamic-update-slice
  16.7 0.8 dynamic-update-slice.3
  17.6 0.8 dynamic-update-slice.6
  18.4 0.8 dynamic-update-slice.2
  19.3 42.2 %all-reduce.16 = (bf16[3072]{0:T(1024)(128)(2,1)}, bf16[768]{0:T(1024)(128)(2,1)}, bf16[768]{0:T(1024)(128)(2,1)}, bf16[768]{0:T(1024)(128)(2,1)}, bf16[2304]{0:...) all-reduce(bf16[3072]{0:T(1024)(128)(2,1)S(1)} %dynamic-update-slic, ...), channel_id=1, replica_groups=mesh['dp'=16,'seq'=2] {'dp','seq'}, use_global_device_ids=true, to_apply=%add.6 | all-reduce | flops 9984 | bytes 39936
  61.4 1.6 constant_dynamic-update-slice_fusion.31
  63.0 1.6 constant_dynamic-update-slice_fusion.30
  64.6 1.6 constant_dynamic-update-slice_fusion.29
  66.2 1.6 constant_dynamic-update-slice_fusion.28
  69.1 0.7 constant_dynamic-update-slice_fusion.25
  70.4 0.7 constant_dynamic-update-slice_fusion.23
  71.1 0.7 constant_dynamic-update-slice_fusion.22
  73.1 0.7 constant_dynamic-update-slice_fusion.19
  73.8 0.7 constant_dynamic-update-slice_fusion.18
  74.4 0.7 constant_dynamic-update-slice_fusion.17
  76.4 0.7 constant_dynamic-update-slice_fusion.14
  79.1 0.7 constant_dynamic-update-slice_fusion.10
  80.5 0.7 constant_dynamic-update-slice_fusion.8
  82.3 0.7 compare_and_fusion
  83.1 1.8 convolution_convert_fusion
  85.0 44.8 %all-gather.4.cloned.1.call-done = bf16[768,2304]{1,0:T(8,128)(2,1)} async-done(((bf16[24,2304]{1,0:T(8,128)(2,1)}), bf16[768,2304]{1,0:T(8,128)(2,1)}) %all-gather.4.cloned.1.call-update) | async-done | bytes 3538960 | tf_op jit(solution)/shard_map/all_gather | solution.py:104
  129.8 2.7 convolution_add_fusion
  132.6 0.8 fusion.77
  133.4 1.1 copy.50
  134.5 0.9 copy.49
  135.5 1.0 slice.128
  136.5 0.9 subtract_convert_fusion
  137.9 2.8 collective-permute-start.2
  141.0 1.3 collective-permute-start
  142.3 0.7 slice_bitcast_fusion
  143.5 1.5 fusion.78
  146.1 1.8 fusion.58
  149.3 0.7 constant_dynamic-update-slice_fusion.4
  151.9 0.7 constant_dynamic-update-slice_fusion
  152.6 3.6 all-to-all-start
  156.9 1.3 collective-permute-start.4
  158.2 0.7 multiply_convert_fusion
  159.2 1.3 collective-permute-start.3
  160.5 1.3 convolution_bitcast_fusion.1
  161.9 0.7 collective-permute-done.3
  163.3 4.1 fusion.69
  168.2 58.0 %all-gather.8.cloned.1.call-done = bf16[768,3072]{1,0:T(8,128)(2,1)} async-done(((bf16[24,3072]{1,0:T(8,128)(2,1)}), bf16[768,3072]{1,0:T(8,128)(2,1)}) %all-gather.8.cloned.1.call-update) | async-done | bytes 4718608 | tf_op jit(solution)/shard_map/all_gather | solution.py:110
  226.2 7.6 %fusion.3 = (bf16[128,3072]{1,0:T(8,128)(2,1)S(1)}, f32[128,3072]{1,0:T(8,128)}) fusion(f32[3072]{0:T(1024)S(1)} %convert_element_type.163, bf16[768,3072]{1,0:T(8,128)(2,1)} %all-gather.8.cloned.1.call-done, bf16[1,128,768]{2,1,0:T(8,128)(2,1)S(1)} %copy-done.1, f32[768]{0:T(1024)S(1)} %convert_element_type.161, f32[768]{0:T(1024)S(1)} %convert_element_type.160, ...), kind=kOutput, calls=%fused_computation.8 | convolution fusion | flops 630521856 | bytes 7293952 | tf_op jit(solution)/shard_map/dot_general | solution.py:194
  233.8 46.3 %all-to-all-done = bf16[32,96,768]{2,1,0:T(8,128)(2,1)} async-done(((bf16[32,96,768]{2,1,0:T(8,128)(2,1)}), bf16[32,96,768]{2,1,0:T(8,128)(2,1)}, u32[]{:S(2)}, u32[]{:S(2)}) %all-to-all-start) | async-done | bytes 4718624 | tf_op jit(solution)/shard_map/all_to_all | solution.py:17
  280.1 4.9 fusion.79
  285.0 5.1 fusion.49
  290.2 5.1 fusion.56
  296.4 4.2 fusion.51
  300.6 1.5 fusion.45
  302.2 1.0 convert_reduce_fusion
  303.1 38.5 %all-reduce.15 = (f32[768]{0:T(1024)S(1)}, f32[768]{0:T(1024)S(1)}, f32[2304]{0:T(1024)S(1)}, f32[768]{0:T(1024)S(1)}, f32[768]{0:T(1024)S(1)}, /*index=5*/f32[768]{0:T(1024)S(1)}, f32[3072]{0:T(1024)S(1)}) all-reduce(f32[768]{0:T(1024)S(1)} %get-tuple-element.16, ...), channel_id=2, replica_groups=mesh['dp'=16,'seq'=2] {'dp','seq'}, use_global_device_ids=true, to_apply=%region_10.11.clone | all-reduce | flops 9216 | bytes 73728
  345.3 3.4 convolution_add_fusion.3
  348.7 1.1 fusion.19
  349.8 108.5 %reduce-scatter.5.cloned.1.call-done = f32[24,2304]{1,0:T(8,128)} async-done(((f32[768,2304]{1,0:T(8,128)}), f32[24,2304]{1,0:T(8,128)}) %reduce-scatter.5.cloned.1.call-update) | async-done | bytes 221200 | tf_op jit(solution)/shard_map/reduce_scatter | solution.py:298
  458.3 141.5 %reduce-scatter.9.cloned.1.call-done = f32[24,3072]{1,0:T(8,128)} async-done(((f32[768,3072]{1,0:T(8,128)}), f32[24,3072]{1,0:T(8,128)}) %reduce-scatter.9.cloned.1.call-update) | async-done | bytes 294928 | tf_op jit(solution)/shard_map/reduce_scatter | solution.py:304
  599.7 141.6 %reduce-scatter.11.cloned.1.call-done = f32[96,768]{1,0:T(8,128)} async-done(((f32[3072,768]{1,0:T(8,128)}), f32[96,768]{1,0:T(8,128)}) %reduce-scatter.11.cloned.1.call-update) | async-done | bytes 294928 | tf_op jit(solution)/shard_map/reduce_scatter | solution.py:306
  (138 shorter events, 22.8 us)
Async XLA Ops:
  7.2 60.6 %copy-start = (bf16[96,768]{1,0:T(8,128)(2,1)S(1)}, bf16[96,768]{1,0:T(8,128)(2,1)}, u32[]{:S(2)}) copy-start(bf16[96,768]{1,0:T(8,128)(2,1)} %param.29) | copy-start | bytes 442372
  7.2 75.9 %all-gather.6.cloned.1.call-start = ((), (), s32[]{:S(2)}) async-start(), calls=%async_computation.6 | async-start | bytes 1216512 | tf_op jit(solution)/shard_map/all_gather | solution.py:106
  7.9 121.9 %all-gather.4.cloned.1.call-start = ((), (), s32[]{:S(2)}) async-start(), calls=%async_computation.5 | async-start | bytes 3649536 | tf_op jit(solution)/shard_map/all_gather | solution.py:104
  8.7 217.5 %all-gather.8.cloned.1.call-start = ((), (), s32[]{:S(2)}) async-start(), calls=%async_computation.7 | async-start | bytes 4866048 | tf_op jit(solution)/shard_map/all_gather | solution.py:110
  9.4 340.3 %reduce-scatter.7.cloned.1.call-start = ((), (), s32[]{:S(2)}) async-start(), calls=%async_computation.9 | async-start | bytes 2433024 | tf_op jit(solution)/shard_map/reduce_scatter | solution.py:300
  10.1 72.2 %collective-permute-start.1 = (bf16[1,128]{1,0:T(2,128)(2,1)S(1)}, bf16[1,128]{1,0:T(2,128)(2,1)S(1)}, u32[]{:S(2)}, u32[]{:S(2)}) collective-permute-start(bf16[1,128]{1,0:T(2,128)(2,1)S(1)} %get-tuple-element.60), channel_id=1, source_target_pairs={{0,1},{2,3},{4,5},{6,7},{8,9},{10,11},{12,13},{14,15},{16,17},{18,... | collective-permute-start | bytes 776 | tf_op jit(solution)/shard_map/ppermute | solution.py:23
  74.4 7.4 copy-start.1
  75.8 6.4 copy-start.19
  75.8 7.3 copy-start.4
  81.9 50.6 %copy-start.10 = (f32[128]{0:T(128)}, f32[128]{0:T(128)S(1)}, u32[]{:S(2)}) copy-start(f32[128]{0:T(128)S(1)} %broadcast_multiply_fusion.4) | copy-start | bytes 1540
  82.1 50.4 %copy-start.12 = (f32[128]{0:T(128)}, f32[128]{0:T(128)S(1)}, u32[]{:S(2)}) copy-start(f32[128]{0:T(128)S(1)} %add_rsqrt_fusion) | copy-start | bytes 1540
  137.3 0.6 copy-start.8
  137.9 5.5 collective-permute-start.2
  141.0 2.4 collective-permute-start
  146.0 1.9 copy-start.5
  152.6 127.5 %all-to-all-start = ((bf16[32,96,768]{2,1,0:T(8,128)(2,1)}), bf16[32,96,768]{2,1,0:T(8,128)(2,1)}, u32[]{:S(2)}, u32[]{:S(2)}) async-start(bf16[32,96,768]{2,1,0:T(8,128)(2,1)} %bitcast.18), calls=%async_computation | async-start | bytes 9437184 | tf_op jit(solution)/shard_map/all_to_all | solution.py:17
  156.2 302.1 %reduce-scatter.5.cloned.1.call-start = ((), (), s32[]{:S(2)}) async-start(), calls=%async_computation.8 | async-start | bytes 7299072 | tf_op jit(solution)/shard_map/reduce_scatter | solution.py:298
  156.9 5.9 collective-permute-start.4
  158.9 1.6 copy-start.7
  158.9 1.6 copy-start.9
  159.2 3.3 collective-permute-start.3
  162.6 0.7 copy-start.11
  162.6 0.7 copy-start.13
  167.4 0.7 copy-start.14
  167.4 0.7 copy-start.18
  167.4 0.7 copy-start.17
  167.5 432.3 %reduce-scatter.9.cloned.1.call-start = ((), (), s32[]{:S(2)}) async-start(), calls=%async_computation.10 | async-start | bytes 9732096 | tf_op jit(solution)/shard_map/reduce_scatter | solution.py:304
  290.2 451.1 %reduce-scatter.11.cloned.1.call-start = ((), (), s32[]{:S(2)}) async-start(), calls=%async_computation.11 | async-start | bytes 9732096 | tf_op jit(solution)/shard_map/reduce_scatter | solution.py:306
  295.3 0.7 copy-start.16
  295.3 0.7 copy-start.15
  296.4 4.2 copy-start.3
  342.9 398.4 %copy-start.20 = (f32[24]{0:T(128)}, f32[24]{0:T(128)S(1)}, u32[]{:S(2)}) copy-start(f32[24]{0:T(128)S(1)} %dynamic-slice.3) | copy-start | bytes 292
  345.2 3.4 copy-start.2
  345.3 3.4 copy-start.6
Sparse Core Ops, SparseCore 0:
  10.9 56.8 all-gather.5
  70.7 59.1 all-gather.3
  132.8 93.3 all-gather.7
  231.9 101.4 reduce-scatter.6
  339.5 118.6 reduce-scatter.4
  464.6 135.0 reduce-scatter.8
  606.2 135.0 reduce-scatter.10
